TPU v7x, 32 devices: a whole 2x2x4 slice. The times are simulated.
32 devices in a mesh: parts: 2 (over x), tok: 16 (over z, y, core).
Axes of the slice: x: 2, y: 2, z: 4, core: 2. Of those that a mesh axis runs over, the one named last changes fastest.
Arguments:
- queries: bfloat16 [4096, 4096], P(('parts', 'tok')), parts along dimension 0, may hold values from -30 to 30
- keys: bfloat16 [4096, 512], P(('parts', 'tok')), parts along dimension 0, may hold values from -4 to 4
- values: bfloat16 [4096, 512], P(('parts', 'tok')), parts along dimension 0, may hold values from -5 to 5
- outputs: bfloat16 [4096, 4096], P(('parts', 'tok')), parts along dimension 0, may hold values from -3 to 3
- out_grad: bfloat16 [4096, 4096], P(('parts', 'tok')), parts along dimension 0, may hold values from -6 to 6
- ancestors: int32 [32, 10], P('parts'), parts along dimension 0, may hold values from -1 to 14, as said below
Outputs:
- query_grad: bfloat16 [4096, 4096], P(('parts', 'tok')), parts along dimension 0
- key_grad: bfloat16 [4096, 512], P(('parts', 'tok')), parts along dimension 0
- value_grad: bfloat16 [4096, 512], P(('parts', 'tok')), parts along dimension 0
There are 2 independent parts, one for each index of `parts`. A program takes and returns all parts, laid end to end along the dimension named above; each array names one. Nothing has to cross between parts.
Inputs may be any that keep to these rules, and one draw needn't show every extreme that they name: Row t lists the ancestor tiles of tile t, from its parent up to tile 0, each once, then -1 to the end. Every listed tile is earlier than t; tile 0 is an ancestor of every other tile and has none; some tile has exactly 10 ancestors.
All inputs are finite; a program needn't handle non-finite values.
Results may differ from a plain program's by a relative error of at most 0.0053.
Values may be sent and summed in bfloat16 or wider, within the bound.
A program may use at most 128 MiB of HBM per device.

v0:
```python
import jax
import jax.numpy as jnp
from jax import lax
from jax.sharding import PartitionSpec as P

QH = 32
KVH = 4
HD = 128
TILE = 128


def pair_lists(ancestor_rows, query_tiles, block_pairs):
    query_count, depth_count = ancestor_rows.shape
    slot_count = depth_count + 1
    key_list = jnp.concatenate([ancestor_rows, query_tiles[:, None]], axis=1).reshape(-1)
    query_slot = jnp.broadcast_to(
        jnp.arange(query_count, dtype=jnp.int32)[:, None], (query_count, slot_count)
    ).reshape(-1)
    self_flag = jnp.broadcast_to(
        jnp.arange(slot_count) == slot_count - 1, (query_count, slot_count)
    ).reshape(-1)
    is_live = key_list >= 0
    ranking = jnp.argsort(1 - is_live.astype(jnp.int32), stable=True)
    pair_total = query_count * slot_count
    padded = -(-pair_total // block_pairs) * block_pairs
    padding_count = padded - pair_total

    def arrange(entries, filler):
        return jnp.concatenate(
            [entries[ranking], jnp.full((padding_count,), filler, entries.dtype)]
        )

    live_pairs = jnp.sum(is_live.astype(jnp.int32))
    return (
        arrange(query_slot, 0),
        arrange(jnp.maximum(key_list, 0), 0),
        arrange(self_flag, False),
        arrange(is_live, False),
        live_pairs,
        padded,
    )


def tree_backward(queries, outputs, out_grad, keys, values, ancestor_rows, query_tiles):
    query_count, tile_len, kv_count, group_len, head_dim = queries.shape
    softmax_scale = head_dim ** (-0.5)
    block_pairs = max(1, 64 // (kv_count * group_len))
    pair_query, pair_key, pair_self, pair_live, live_pairs, padded = pair_lists(
        ancestor_rows, query_tiles, block_pairs
    )
    block_total = (live_pairs + block_pairs - 1) // block_pairs
    causal = jnp.arange(tile_len)[:, None] >= jnp.arange(tile_len)[None, :]

    def take_block(index):
        start = index * block_pairs
        return tuple(
            (
                lax.dynamic_slice_in_dim(entry, start, block_pairs)
                for entry in (pair_query, pair_key, pair_self, pair_live)
            )
        )

    def masked_scores(query_block, key_block, self_ids, live_ids):
        raw_scores = (
            jnp.einsum(
                "bikgd,bjkd->bkgij", query_block, key_block, preferred_element_type=jnp.float32
            )
            * softmax_scale
        )
        key_mask = live_ids[:, None, None] & (
            jnp.logical_not(self_ids)[:, None, None] | causal[None]
        )
        return jnp.where(key_mask[:, None, None], raw_scores, -1e30)

    stat_shape = (padded, kv_count, group_len, tile_len)

    def first_sweep(index, state):
        max_rows, sum_rows = state
        query_ids, key_ids, self_ids, live_ids = take_block(index)
        masked = masked_scores(queries[query_ids], keys[key_ids], self_ids, live_ids)
        block_max = jnp.max(masked, axis=-1)
        block_sum = (
            jnp.sum(jnp.exp(masked - block_max[..., None]), axis=-1)
            * live_ids.astype(jnp.float32)[:, None, None, None]
        )
        start = index * block_pairs
        return (
            lax.dynamic_update_slice_in_dim(max_rows, block_max, start, 0),
            lax.dynamic_update_slice_in_dim(sum_rows, block_sum, start, 0),
        )

    max_rows, sum_rows = lax.fori_loop(
        0,
        block_total,
        first_sweep,
        (jnp.full(stat_shape, -1e30, jnp.float32), jnp.zeros(stat_shape, jnp.float32)),
    )
    row_shape = (query_count, kv_count, group_len, tile_len)
    row_max = jnp.full(row_shape, -1e30, jnp.float32).at[pair_query].max(max_rows)
    row_total = (
        jnp.zeros(row_shape, jnp.float32)
        .at[pair_query]
        .add(sum_rows * jnp.exp(max_rows - row_max[pair_query]))
    )
    log_total = row_max + jnp.log(row_total)
    row_delta = jnp.transpose(
        jnp.sum(out_grad.astype(jnp.float32) * outputs.astype(jnp.float32), axis=-1), (0, 2, 3, 1)
    )

    def second_sweep(index, state):
        query_acc, key_acc, value_acc = state
        query_ids, key_ids, self_ids, live_ids = take_block(index)
        query_block = queries[query_ids]
        key_block = keys[key_ids]
        value_block = values[key_ids]
        grad_block = out_grad[query_ids]
        masked = masked_scores(query_block, key_block, self_ids, live_ids)
        attn_probs = jnp.exp(masked - log_total[query_ids][..., None])
        grad_probs = jnp.einsum(
            "bikgd,bjkd->bkgij", grad_block, value_block, preferred_element_type=jnp.float32
        )
        grad_scores = (attn_probs * (grad_probs - row_delta[query_ids][..., None])).astype(
            jnp.bfloat16
        )
        probs_low = attn_probs.astype(jnp.bfloat16)
        query_acc = query_acc.at[query_ids].add(
            jnp.einsum(
                "bkgij,bjkd->bikgd", grad_scores, key_block, preferred_element_type=jnp.float32
            )
        )
        key_acc = key_acc.at[key_ids].add(
            jnp.einsum(
                "bkgij,bikgd->bjkd", grad_scores, query_block, preferred_element_type=jnp.float32
            )
        )
        value_acc = value_acc.at[key_ids].add(
            jnp.einsum(
                "bkgij,bikgd->bjkd", probs_low, grad_block, preferred_element_type=jnp.float32
            )
        )
        return (query_acc, key_acc, value_acc)

    start_state = (
        jnp.zeros(queries.shape, jnp.float32),
        jnp.zeros(keys.shape, jnp.float32),
        jnp.zeros(keys.shape, jnp.float32),
    )
    query_acc, key_acc, value_acc = lax.fori_loop(0, block_total, second_sweep, start_state)
    return ((query_acc * softmax_scale).astype(jnp.bfloat16), key_acc, value_acc)


def per_device(queries, keys, values, outputs, out_grad, ancestors):
    tile_count = ancestors.shape[0]
    groups = QH // KVH
    row_count = queries.shape[0]
    tiles_here = row_count // TILE
    softmax_scale = HD ** (-0.5)
    gathered_keys, gathered_values = (
        lax.all_gather(keys, "tok", axis=0, tiled=True),
        lax.all_gather(values, "tok", axis=0, tiled=True),
    )
    first_tile = lax.axis_index("tok") * tiles_here
    query_tiles = first_tile + jnp.arange(tiles_here, dtype=jnp.int32)
    ancestor_rows = lax.dynamic_slice_in_dim(ancestors, first_tile, tiles_here, 0)
    query_shape = (tiles_here, TILE, KVH, groups, HD)
    key_shape = (tile_count, TILE, KVH, HD)
    query_grad, key_acc, value_acc = tree_backward(
        queries.reshape(query_shape),
        outputs.reshape(query_shape),
        out_grad.reshape(query_shape),
        gathered_keys.reshape(key_shape),
        gathered_values.reshape(key_shape),
        ancestor_rows,
        query_tiles,
    )
    all_rows = tile_count * TILE
    key_sum, value_sum = (
        lax.psum_scatter(
            key_acc.reshape(all_rows, KVH * HD), "tok", scatter_dimension=0, tiled=True
        ),
        lax.psum_scatter(
            value_acc.reshape(all_rows, KVH * HD), "tok", scatter_dimension=0, tiled=True
        ),
    )
    return (
        query_grad.reshape(row_count, QH * HD),
        (key_sum * softmax_scale).astype(jnp.bfloat16),
        value_sum.astype(jnp.bfloat16),
    )


def solution(mesh):
    return jax.shard_map(
        per_device,
        mesh=mesh,
        in_specs=(
            P(("parts", "tok"), None),
            P(("parts", "tok"), None),
            P(("parts", "tok"), None),
            P(("parts", "tok"), None),
            P(("parts", "tok"), None),
            P("parts", None),
        ),
        out_specs=(P(("parts", "tok"), None), P(("parts", "tok"), None), P(("parts", "tok"), None)),
        check_vma=False,
    )
```

profile of v0, /device:TPU:0, one launch (start us, length us, event | category | flops | bytes accessed | tf_op | source)
XLA Modules:
  0.0 461.3 jit_solution(17456207643026106930)
XLA Ops:
  14.2 1.6 copy.23
  16.5 1.6 copy.26
  18.1 1.6 copy.25
  19.7 1.3 copy.28
  21.7 32.6 %all-gather.3.cloned.1.call-done = bf16[2048,512]{1,0:T(8,128)(2,1)} async-done(((bf16[128,512]{1,0:T(8,128)(2,1)}), bf16[2048,512]{1,0:T(8,128)(2,1)}) %all-gather.3.cloned.1.call-update) | async-done | bytes 2097168 | tf_op jit(solution)/shard_map/all_gather | solution.py:159
  54.3 2.5 reshape.152
  58.2 3.8 while.30
  62.0 2.1 scatter_fusion.3
  66.2 30.4 %all-gather.5.cloned.1.call-done = bf16[2048,512]{1,0:T(8,128)(2,1)} async-done(((bf16[128,512]{1,0:T(8,128)(2,1)}), bf16[2048,512]{1,0:T(8,128)(2,1)}) %all-gather.5.cloned.1.call-update) | async-done | bytes 2097168 | tf_op jit(solution)/shard_map/all_gather | solution.py:160
  96.7 4.0 reshape.154
  100.9 2.4 broadcast.103.clone
  103.3 2.5 broadcast.103
  105.8 31.9 %while.29 = (s32[]{:T(128)}, f32[1,128,4,8,128]{4,3,2,1,0:T(8,128)S(1)}, f32[16,128,4,128]{3,1,2,0:T(8,128)}, f32[16,128,4,128]{3,1,2,0:T(8,128)}, s32[]{:T(128)...) while((s32[]{:T(128)}, ...), condition=%wide.region_13.14_spmd.clone, body=%wide.region_9.13_spmd.clone.sunk | while | flops 1354056704 | bytes 60215672 | solution.py:148
  106.2 3.1 gather_fusion.1
  109.2 3.1 gather_fusion
  114.7 1.9 fusion.61
  116.6 1.5 fusion.60
  118.1 1.6 convolution_bitcast_fusion.5
  119.6 2.7 convolution_bitcast_fusion.4
  122.3 5.5 %copy.64 = f32[2,128,4,8,128]{4,3,2,1,0:T(8,128)} copy(f32[2,128,4,8,128]{1,4,3,2,0:T(8,128)} %convolution_bitcast_fusion.4) | data formatting | bytes 8388608 | tf_op jit(solution)/shard_map/while/body/bkgij,bjkd->bikgd/transpose | solution.py:127
  127.7 4.8 %scatter_fusion = f32[128,4,8,128,1]{3,2,4,1,0:T(8,128)S(1)} fusion(f32[128,4,8,128,1]{3,2,4,1,0:T(8,128)S(1)} %bitcast.130, s32[2]{0:T(128)S(1)} %get-tuple-element.464, f32[2,128,4,8,128]{4,3,2,1,0:T(8,128)} %copy.64), kind=kCustom, calls=%fused_computation.7.clone.clone.1 | custom fusion | flops 1048576 | bytes 12582920 | tf_op jit(solution)/shard_map/while/body/scatter-add | solution.py:126
  132.5 2.6 scatter_fusion.1
  135.1 2.6 scatter_fusion.2
  137.8 5.0 %copy.30 = f32[16,128,4,128]{3,2,1,0:T(4,128)S(1)} copy(f32[16,128,4,128]{3,1,2,0:T(8,128)} %get-tuple-element.153) | data formatting | bytes 8388608 | tf_op jit(solution)/shard_map/while | solution.py:148
  142.7 2.4 copy.56
  145.4 5.0 %copy.29 = f32[16,128,4,128]{3,2,1,0:T(4,128)S(1)} copy(f32[16,128,4,128]{3,1,2,0:T(8,128)} %get-tuple-element.152) | data formatting | bytes 8388608 | tf_op jit(solution)/shard_map/while | solution.py:148
  150.4 2.4 copy.57
  153.1 1.3 reshape.156
  154.4 223.1 %reduce-scatter.5.cloned.1.call-done = f32[128,512]{1,0:T(8,128)} async-done(((f32[2048,512]{1,0:T(8,128)}), f32[128,512]{1,0:T(8,128)}) %reduce-scatter.5.cloned.1.call-update) | async-done | bytes 262160 | tf_op jit(solution)/shard_map/reduce_scatter | solution.py:181
  377.4 1.6 convert_element_type.53
  379.1 74.1 %reduce-scatter.3.cloned.1.call-done = f32[128,512]{1,0:T(8,128)} async-done(((f32[2048,512]{1,0:T(8,128)}), f32[128,512]{1,0:T(8,128)}) %reduce-scatter.3.cloned.1.call-update) | async-done | bytes 262160 | tf_op jit(solution)/shard_map/reduce_scatter | solution.py:178
  453.1 1.6 multiply_convert_fusion.1
  (64 shorter events, 18.3 us)
Async XLA Ops:
  7.2 1.6 copy-start
  7.2 47.1 %all-gather.3.cloned.1.call-start = ((), (), s32[]{:S(2)}) async-start(), calls=%async_computation.2 | async-start | bytes 2228224 | tf_op jit(solution)/shard_map/all_gather | solution.py:159
  7.9 88.7 %all-gather.5.cloned.1.call-start = ((), (), s32[]{:S(2)}) async-start(), calls=%async_computation.3 | async-start | bytes 2228224 | tf_op jit(solution)/shard_map/all_gather | solution.py:160
  8.7 368.8 %reduce-scatter.5.cloned.1.call-start = ((), (), s32[]{:S(2)}) async-start(), calls=%async_computation.5 | async-start | bytes 4456448 | tf_op jit(solution)/shard_map/reduce_scatter | solution.py:181
  62.0 38.6 %copy-start.2 = (bf16[16,128,4,128]{3,2,1,0:T(4,128)(2,1)}, bf16[16,128,4,128]{3,2,1,0:T(4,128)(2,1)S(1)}, u32[]{:S(2)}) copy-start(bf16[16,128,4,128]{3,2,1,0:T(4,128)(2,1)S(1)} %get-tuple-element.586) | copy-start | bytes 6291460
  113.4 1.2 copy-start.4
  114.7 1.9 copy-start.3
  145.1 308.0 %reduce-scatter.3.cloned.1.call-start = ((), (), s32[]{:S(2)}) async-start(), calls=%async_computation.4 | async-start | bytes 4456448 | tf_op jit(solution)/shard_map/reduce_scatter | solution.py:178
  152.8 302.0 %copy-start.1 = (s32[16,10]{1,0:T(8,128)S(1)}, s32[16,10]{1,0:T(8,128)}, u32[]{:S(2)}) copy-start(s32[16,10]{1,0:T(8,128)} %param.15) | copy-start | bytes 1924
Sparse Core Ops, SparseCore 0:
  10.2 44.0 all-gather.2
  56.4 40.1 all-gather.4
  145.2 232.1 reduce-scatter.4
  381.6 71.4 reduce-scatter.2
where the time goes:
time: 464 us; the launch traced here: 461 us
  waiting for transfers between devices  362 us (78%)
  local copies, waits for them, and re-layouts  52.7 us (11%)
  other arithmetic  22.8 us (5%)
  between operations  14.6 us (3%)
  matrix products  9.12 us (2%)
    reduce_scatter x1, waiting for transfers between devices, per_device(): lax.psum_scatter(value_acc.reshape(all_rows, KVH * HD), 'tok', scatter_di...  223 us
    reduce_scatter x1, waiting for transfers between devices, per_device(): lax.psum_scatter(key_acc.reshape(all_rows, KVH * HD), 'tok', scatter_dime...  74.1 us
    all_gather x1, waiting for transfers between devices, per_device(): lax.all_gather(keys, 'tok', axis=0, tiled=True)  32.6 us
    all_gather x1, waiting for transfers between devices, per_device(): lax.all_gather(values, 'tok', axis=0, tiled=True)  30.4 us
    unnamed x13, local copies, waits for them, and re-layouts  11.6 us
    while x2, local copies, waits for them, and re-layouts, tree_backward(): lax.fori_loop(0, block_total, second_sweep, start_state)  9.95 us
  transfers between devices with their start and end apart: 4, of which 4 were waited for; matrix products, arithmetic and copies ran while one was open for 8% of the time, Pallas kernels for 0%

commit v1 on v0

v1 whole, which is shorter than its diff:
```python
import functools
import math

import jax
import jax.numpy as jnp
from jax import lax
from jax.experimental import pallas as pl
from jax.experimental.pallas import tpu as pltpu
from jax.sharding import PartitionSpec as P

QH = 32
KVH = 4
HD = 128
TILE = 128
GROUP = QH // KVH
ROWS = GROUP * TILE
SCALE = HD ** -0.5
EXP_SCALE = SCALE * math.log2(math.e)
LOOP = lax.fori_loop
NY = 2
NC = 2


class Place:
    def __init__(self, tiles):
        self.nz = tiles // (NY * NC)
        tok = lax.axis_index("tok")
        self.me = tok
        self.z = tok // (NY * NC)
        self.y = lax.rem(tok // NC, NY)
        self.c = lax.rem(tok, NC)

    def at(self, z, y, c):
        return {"tok": (z * NY + y) * NC + c}

    def meet(self):
        barrier = pltpu.get_barrier_semaphore()

        def greet(d, carry):
            pl.semaphore_signal(
                barrier, 1, device_id=self.at(lax.rem(self.z + d, self.nz), self.y, self.c)
            )
            return carry

        LOOP(1, self.nz, greet, 0)
        pl.semaphore_signal(barrier, 1, device_id=self.at(self.z, 1 - self.y, self.c))
        pl.semaphore_signal(barrier, 1, device_id=self.at(self.z, self.y, 1 - self.c))
        pl.semaphore_wait(barrier, self.nz + 1)


def each(start, stop, body):
    def step(i, carry):
        body(i)
        return carry

    LOOP(start, stop, step, 0)


class Gather:
    def __init__(self, place, buf, sems):
        self.p, self.buf = place, buf
        self.zs, self.zr, self.ys, self.yr, self.cs, self.cr = sems

    @staticmethod
    def sems(nz):
        dma = pltpu.SemaphoreType.DMA
        return [
            dma((KVH, nz)), dma((KVH, nz)), dma((KVH, nz)), dma((KVH, nz)),
            dma((KVH, NY, nz)), dma((KVH, NY, nz)),
        ]

    def to_plane(self, g, src_z, dst_z):
        p = self.p
        block = self.buf.at[g, src_z, p.y, p.c]
        return pltpu.make_async_remote_copy(
            block, block, self.zs.at[g, dst_z], self.zr.at[g, src_z],
            device_id=p.at(dst_z, p.y, p.c))

    def to_y(self, g, z, y):
        p = self.p
        block = self.buf.at[g, z, y, p.c]
        return pltpu.make_async_remote_copy(
            block, block, self.ys.at[g, z], self.yr.at[g, z],
            device_id=p.at(p.z, 1 - p.y, p.c))

    def to_core(self, g, z, y, c):
        p = self.p
        block = self.buf.at[g, z, y, c]
        return pltpu.make_async_remote_copy(
            block, block, self.cs.at[g, y, z], self.cr.at[g, y, z],
            device_id=p.at(p.z, p.y, 1 - p.c))

    def first(self, g):
        p = self.p
        self.to_y(g, p.z, p.y).start()
        self.to_core(g, p.z, p.y, p.c).start()
        each(p.z + 1, p.nz, lambda dz: self.to_plane(g, p.z, dz).start())

    def second(self, g):
        p = self.p

        def step(z):
            self.to_plane(g, z, p.z).wait_recv()
            self.to_y(g, z, p.y).start()
            self.to_core(g, z, p.y, p.c).start()

        each(0, p.z, step)

    def third(self, g):
        p = self.p

        def step(z):
            self.to_y(g, z, 1 - p.y).wait_recv()
            self.to_core(g, z, 1 - p.y, p.c).start()

        each(0, p.z + 1, step)

    def fourth(self, g):
        p = self.p

        def step(z):
            self.to_core(g, z, 0, 1 - p.c).wait_recv()
            self.to_core(g, z, 1, 1 - p.c).wait_recv()

        each(0, p.z + 1, step)

    def drain(self, g):
        p = self.p
        each(p.z + 1, p.nz, lambda dz: self.to_plane(g, p.z, dz).wait_send())

        def step(z):
            self.to_y(g, z, p.y).wait_send()
            self.to_core(g, z, 0, p.c).wait_send()
            self.to_core(g, z, 1, p.c).wait_send()

        each(0, p.z + 1, step)


class Reduce:
    def __init__(self, place, part, scratch):
        self.p, self.part = place, part
        (self.from_core, self.for_y, self.from_y, self.for_z, self.from_z, self.own,
         self.cs, self.cr, self.ys, self.yr, self.zs, self.zr) = scratch

    @staticmethod
    def scratch(nz):
        dma = pltpu.SemaphoreType.DMA
        block = (2, TILE, HD)
        return [
            pltpu.VMEM((KVH, nz, NY) + block, jnp.bfloat16),
            pltpu.VMEM((KVH, nz) + block, jnp.bfloat16),
            pltpu.VMEM((KVH, nz) + block, jnp.bfloat16),
            pltpu.VMEM((KVH, nz) + block, jnp.bfloat16),
            pltpu.VMEM((KVH, nz) + block, jnp.bfloat16),
            pltpu.VMEM((KVH,) + block, jnp.float32),
        ] + [dma((KVH, NY, nz))] * 2 + [dma((KVH, nz))] * 4

    def to_core(self, g, z, y):
        p = self.p
        return pltpu.make_async_remote_copy(
            self.part.at[g, z, y, 1 - p.c], self.from_core.at[g, z, y],
            self.cs.at[g, y, z], self.cr.at[g, y, z],
            device_id=p.at(p.z, p.y, 1 - p.c))

    def to_y(self, g, z):
        p = self.p
        return pltpu.make_async_remote_copy(
            self.for_y.at[g, z], self.from_y.at[g, z], self.ys.at[g, z], self.yr.at[g, z],
            device_id=p.at(p.z, 1 - p.y, p.c))

    def to_plane(self, g, src_z, dst_z):
        p = self.p
        return pltpu.make_async_remote_copy(
            self.for_z.at[g, dst_z], self.from_z.at[g, src_z],
            self.zs.at[g, dst_z], self.zr.at[g, src_z],
            device_id=p.at(dst_z, p.y, p.c))

    def first(self, g):
        p = self.p

        def step(z):
            self.to_core(g, z, 1 - p.y).start()
            self.to_core(g, z, p.y).start()

        each(0, p.z + 1, step)

    def second(self, g):
        p = self.p

        def step(z):
            y = 1 - p.y
            self.to_core(g, z, y).wait_recv()
            total = self.part[g, z, y, p.c].astype(jnp.float32) + self.from_core[g, z, y].astype(jnp.float32)
            self.for_y[g, z] = total.astype(jnp.bfloat16)
            self.to_y(g, z).start()

        each(0, p.z + 1, step)

    def third(self, g):
        p = self.p

        def total(z):
            self.to_core(g, z, p.y).wait_recv()
            self.to_y(g, z).wait_recv()
            return (
                self.part[g, z, p.y, p.c].astype(jnp.float32)
                + self.from_core[g, z, p.y].astype(jnp.float32)
                + self.from_y[g, z].astype(jnp.float32)
            )

        def step(z):
            self.for_z[g, z] = total(z).astype(jnp.bfloat16)
            self.to_plane(g, p.z, z).start()

        each(0, p.z, step)
        self.own[g] = total(p.z)

    def fourth(self, g):
        p = self.p

        def step(z):
            self.to_plane(g, z, p.z).wait_recv()
            self.own[g] += self.from_z[g, z].astype(jnp.float32)

        each(p.z + 1, p.nz, step)

    def drain(self, g):
        p = self.p

        def step(z):
            self.to_core(g, z, 0).wait_send()
            self.to_core(g, z, 1).wait_send()
            self.to_y(g, z).wait_send()

        each(0, p.z + 1, step)
        each(0, p.z, lambda z: self.to_plane(g, p.z, z).wait_send())


def gather_kernel(tiles, k_ref, v_ref, buf, *sems):
    place = Place(tiles)
    gather = Gather(place, buf, sems)
    for g in range(KVH):
        columns = slice(g * HD, (g + 1) * HD)
        buf[g, place.z, place.y, place.c, 0] = k_ref[:, columns]
        buf[g, place.z, place.y, place.c, 1] = v_ref[:, columns]
    place.meet()
    heads = lambda step: each(0, KVH, step)
    heads(gather.first)
    heads(gather.second)
    heads(gather.third)
    heads(gather.fourth)
    heads(gather.drain)


def reduce_kernel(tiles, part, dk_ref, dv_ref, *scratch):
    place = Place(tiles)
    reduce = Reduce(place, part, scratch)
    place.meet()
    heads = lambda step: each(0, KVH, step)
    heads(reduce.first)
    heads(reduce.second)
    heads(reduce.third)
    heads(reduce.fourth)
    heads(reduce.drain)
    for g in range(KVH):
        columns = slice(g * HD, (g + 1) * HD)
        dk_ref[:, columns] = reduce.own[g, 0].astype(jnp.bfloat16)
        dv_ref[:, columns] = reduce.own[g, 1].astype(jnp.bfloat16)


def dot(a, b):
    return jnp.dot(a, b, preferred_element_type=jnp.float32)


def fold(x, op):
    return op(x.reshape(TILE // 8, 8, x.shape[-1]), axis=0)


def compute_kernel(
    table, q_ref, o_ref, g_ref, kv_ref, dq_ref, part_ref,
    qt, qs, gt, gs, delta, scores, peak, total, dqt,
):
    live = table[0]
    part_ref[...] = jnp.zeros_like(part_ref)
    for h in range(GROUP):
        columns = slice(h * TILE, (h + 1) * TILE)
        q, g = q_ref[:, columns], g_ref[:, columns]
        qs[columns, :] = q
        gs[columns, :] = g
        qt[:, columns] = q.T
        gt[:, columns] = g.T
        product = g.astype(jnp.float32) * o_ref[:, columns].astype(jnp.float32)
        delta[:, columns] = jnp.sum(product.T, axis=0, keepdims=True)

    own = table[1]
    s = dot(kv_ref[0, own, 0], qt[...])
    key_pos = lax.broadcasted_iota(jnp.int32, s.shape, 0)
    query_pos = lax.broadcasted_iota(jnp.int32, s.shape, 1) & (TILE - 1)
    s = jnp.where(key_pos <= query_pos, s, -1e30)
    scores[0] = s
    peak[...] = fold(s, jnp.max)

    def score(i):
        s = dot(kv_ref[0, table[1 + i], 0], qt[...])
        scores[i] = s
        peak[...] = jnp.maximum(peak[...], fold(s, jnp.max))

    each(1, live, score)
    top = jnp.max(peak[...], axis=0, keepdims=True)
    total[...] = jnp.zeros_like(total)

    def weigh(i):
        w = jnp.exp2((scores[i] - top) * EXP_SCALE)
        scores[i] = w
        total[...] += fold(w, jnp.sum)

    each(0, live, weigh)
    inverse = 1.0 / jnp.sum(total[...], axis=0, keepdims=True)
    dqt[...] = jnp.zeros_like(dqt)

    def back(i):
        tile = table[1 + i]
        k = kv_ref[0, tile, 0]
        p = scores[i] * inverse
        dp = dot(kv_ref[0, tile, 1], gt[...])
        ds = (p * (dp - delta[...])).astype(jnp.bfloat16)
        part_ref[0, tile, 1] = dot(p.astype(jnp.bfloat16), gs[...]).astype(jnp.bfloat16)
        part_ref[0, tile, 0] = (dot(ds, qs[...]) * SCALE).astype(jnp.bfloat16)
        dqt[...] += dot(k.T, ds)

    each(0, live, back)
    for h in range(GROUP):
        columns = slice(h * TILE, (h + 1) * TILE)
        dq_ref[:, columns] = (dqt[:, columns].T * SCALE).astype(jnp.bfloat16)


def per_device(tiles, queries, keys, values, outputs, out_grad, ancestors):
    depth = ancestors.shape[1]
    nz = tiles // (NY * NC)
    grid_shape = (KVH, nz, NY, NC, 2, TILE, HD)
    flat_shape = (KVH, tiles, 2, TILE, HD)
    vmem = pl.BlockSpec(memory_space=pltpu.VMEM)
    limit = 56 << 20
    gathered = pl.pallas_call(
        functools.partial(gather_kernel, tiles),
        out_shape=jax.ShapeDtypeStruct(grid_shape, jnp.bfloat16),
        in_specs=[vmem, vmem],
        out_specs=vmem,
        scratch_shapes=Gather.sems(nz),
        compiler_params=pltpu.CompilerParams(
            collective_id=0, has_side_effects=True, vmem_limit_bytes=limit),
    )(keys, values).reshape(flat_shape)

    me = lax.axis_index("tok").astype(jnp.int32)
    row = lax.dynamic_slice_in_dim(ancestors, me, 1, 0)[0]
    table = jnp.concatenate([(1 + jnp.sum((row >= 0).astype(jnp.int32)))[None], me[None], row])
    wide = pl.BlockSpec((TILE, ROWS), lambda g, t: (0, g))
    tall = pl.BlockSpec((1, tiles, 2, TILE, HD), lambda g, t: (g, 0, 0, 0, 0))
    f32, bf16 = jnp.float32, jnp.bfloat16
    query_grad, part = pl.pallas_call(
        compute_kernel,
        out_shape=(
            jax.ShapeDtypeStruct((TILE, QH * HD), bf16),
            jax.ShapeDtypeStruct(flat_shape, bf16),
        ),
        grid_spec=pltpu.PrefetchScalarGridSpec(
            num_scalar_prefetch=1,
            grid=(KVH,),
            in_specs=[wide, wide, wide, tall],
            out_specs=(wide, tall),
            scratch_shapes=[
                pltpu.VMEM((HD, ROWS), bf16),
                pltpu.VMEM((ROWS, HD), bf16),
                pltpu.VMEM((HD, ROWS), bf16),
                pltpu.VMEM((ROWS, HD), bf16),
                pltpu.VMEM((1, ROWS), f32),
                pltpu.VMEM((depth + 1, TILE, ROWS), f32),
                pltpu.VMEM((8, ROWS), f32),
                pltpu.VMEM((8, ROWS), f32),
                pltpu.VMEM((HD, ROWS), f32),
            ],
        ),
        compiler_params=pltpu.CompilerParams(vmem_limit_bytes=limit),
    )(table, queries, outputs, out_grad, gathered)

    key_grad, value_grad = pl.pallas_call(
        functools.partial(reduce_kernel, tiles),
        out_shape=(jax.ShapeDtypeStruct(keys.shape, bf16),) * 2,
        in_specs=[vmem],
        out_specs=(vmem, vmem),
        scratch_shapes=Reduce.scratch(nz),
        compiler_params=pltpu.CompilerParams(
            collective_id=1, has_side_effects=True, vmem_limit_bytes=limit),
    )(part.reshape(grid_shape))
    return query_grad, key_grad, value_grad


def solution(mesh):
    rows = P(("parts", "tok"), None)
    return jax.shard_map(
        functools.partial(per_device, mesh.shape["tok"]),
        mesh=mesh,
        in_specs=(rows,) * 5 + (P("parts", None),),
        out_specs=(rows,) * 3,
        check_vma=False,
    )
```

time: 464 us -> 119 us (0.26)
  waiting for transfers between devices: 362 us -> 0 us
  Pallas kernels: 0 us -> 111 us
  local copies, waits for them, and re-layouts: 52.7 us -> 3.14 us
  other arithmetic: 22.8 us -> 1.93 us
  between operations: 14.6 us -> 1.3 us
  matrix products: 9.12 us -> 0 us
    reduce_scatter x2 -> x0, waiting for transfers between devices: 297 us -> none  [the longest x1 223 us: per_device(): lax.psum_scatter(value_acc.reshape(all_rows, KVH * HD), 'tok', scatter_di...]
    pallas_call x0 -> x3, Pallas kernels: none -> 111 us  [the longest x1 76.6 us: per_device(): pl.pallas_call(functools.partial(reduce_kernel, tiles), out_shape=(jax.Sh...]
    all_gather x2 -> x0, waiting for transfers between devices: 63 us -> none  [the longest x1 32.6 us: per_device(): lax.all_gather(keys, 'tok', axis=0, tiled=True)]
    scatter-add x4 -> x0, other arithmetic: 11.1 us -> none  [the longest x1 4.79 us: second_sweep(): query_acc.at[query_ids]]
    gather x8 -> x0, local copies, waits for them, and re-layouts: 10.7 us -> none  [the longest x2 4.19 us: second_sweep(): key_block = keys[key_ids]]
    while x6 -> x0, local copies, waits for them, and re-layouts: 10.4 us -> none  [the longest x2 9.95 us: tree_backward(): lax.fori_loop(0, block_total, second_sweep, start_state)]
    dot_general x6 -> x0, matrix products: 9.12 us -> none  [the longest x1 2.67 us: second_sweep(): jnp.einsum('bkgij,bjkd->bikgd', grad_scores, key_block, preferred_element...]
    unnamed x13 -> x2, local copies, waits for them, and re-layouts: 11.6 us -> 3.14 us
  transfers between devices with their start and end apart: 4 -> 0, of which waited for: 4 -> 0; matrix products, arithmetic and copies ran while one was open for 8% -> 0% of each run, Pallas kernels for 0% -> 0%
where the time goes in v1:
time: 119 us; the launch traced here: 118 us
  Pallas kernels  111 us (93%)
  local copies, waits for them, and re-layouts  3.14 us (3%)
  other arithmetic  1.93 us (2%)
  between operations  1.3 us (1%)
    pallas_call x1, Pallas kernels, per_device(): pl.pallas_call(functools.partial(reduce_kernel, tiles), out_shape=(jax.Sh...  76.6 us
    pallas_call x1, Pallas kernels, per_device(): pl.pallas_call(functools.partial(gather_kernel, tiles), out_shape=jax.Sha...  26 us
    pallas_call x1, Pallas kernels, per_device(): pl.pallas_call(compute_kernel, out_shape=(jax.ShapeDtypeStruct((TILE, QH...  8.94 us
    unnamed x2, local copies, waits for them, and re-layouts  3.14 us

profile of v1, /device:TPU:0, one launch (start us, length us, event | category | flops | bytes accessed | tf_op | source)
XLA Modules:
  0.0 117.9 jit_solution(9361465483165709981)
XLA Ops:
  0.6 1.3 %fusion = (s32[]{:T(128)}, s32[10]{0:T(128)S(1)}) fusion(s32[16,10]{1,0:T(8,128)} %param.11, s32[]{:T(128)S(6)} %select_n.3), kind=kLoop, calls=%fused_computation.1 | loop fusion | flops 29 | bytes 88 | tf_op jit(solution)/shard_map/reduce_sum | solution.py:356
  2.6 0.6 pad_add_fusion.table
  3.2 26.0 %shard_map.85 = bf16[4,4,2,2,2,128,128]{6,5,4,3,2,1,0:T(8,128)(2,1)} custom-call(bf16[128,512]{1,0:T(8,128)(2,1)} %k_ref.1, bf16[128,512]{1,0:T(8,128)(2,1)} %v_ref.1), custom_call_target="tpu_custom_call" | custom-call | tf_op jit(solution)/shard_map/pallas_call | solution.py:344
  29.2 8.9 %shard_map.86 = (bf16[128,4096]{1,0:T(8,128)(2,1)}, bf16[4,16,2,128,128]{4,3,2,1,0:T(8,128)(2,1)}) custom-call(s32[12]{0:T(128)} %pad_add_fusion.table, bf16[128,4096]{1,0:T(8,128)(2,1)} %q_ref.1, bf16[128,4096]{1,0:T(8,128)(2,1)} %o_ref.1, bf16[128,4096]{1,0:T(8,128)(2,1)} %g_ref.1, bf16[4,16,2,128,128]{4,3,2,1,0:T(8,128)(2,1)} %bitcast.7), custom_call_target="tpu_custom_call" | custom-call | tf_op jit(solution)/shard_map/pallas_call | solution.py:360
  38.2 76.6 %shard_map.87 = (bf16[128,512]{1,0:T(8,128)(2,1)}, bf16[128,512]{1,0:T(8,128)(2,1)}) custom-call(bf16[4,4,2,2,2,128,128]{6,5,4,3,2,1,0:T(8,128)(2,1)} %bitcast.8), custom_call_target="tpu_custom_call" | custom-call | tf_op jit(solution)/shard_map/pallas_call | solution.py:386
  114.7 1.6 %copy.11 = bf16[128,512]{1,0:T(8,128)(2,1)} copy(bf16[128,512]{1,0:T(8,128)(2,1)} %get-tuple-element.17) | data formatting | bytes 262144
  116.3 1.6 %copy.12 = bf16[128,512]{1,0:T(8,128)(2,1)} copy(bf16[128,512]{1,0:T(8,128)(2,1)} %get-tuple-element.18) | data formatting | bytes 262144

commit v2 on v1

v2 whole, which is shorter than its diff:
```python
import functools
import math

import jax
import jax.numpy as jnp
from jax import lax
from jax.experimental import pallas as pl
from jax.experimental.pallas import tpu as pltpu
from jax.sharding import PartitionSpec as P

QH = 32
KVH = 4
HD = 128
TILE = 128
GROUP = QH // KVH
ROWS = GROUP * TILE
SCALE = HD ** -0.5
EXP_SCALE = SCALE * math.log2(math.e)
LOOP = lax.fori_loop
NY = 2
NC = 2


class Place:
    def __init__(self, tiles):
        self.nz = tiles // (NY * NC)
        tok = lax.axis_index("tok")
        self.me = tok
        self.z = tok // (NY * NC)
        self.y = lax.rem(tok // NC, NY)
        self.c = lax.rem(tok, NC)

    def tile(self, z, y, c):
        return (z * NY + y) * NC + c

    def at(self, z, y, c):
        return {"tok": self.tile(z, y, c)}

    def meet(self):
        barrier = pltpu.get_barrier_semaphore()

        def greet(d, carry):
            pl.semaphore_signal(
                barrier, 1, device_id=self.at(lax.rem(self.z + d, self.nz), self.y, self.c)
            )
            return carry

        LOOP(1, self.nz, greet, 0)
        pl.semaphore_signal(barrier, 1, device_id=self.at(self.z, 1 - self.y, self.c))
        pl.semaphore_signal(barrier, 1, device_id=self.at(self.z, self.y, 1 - self.c))
        pl.semaphore_wait(barrier, self.nz + 1)


def each(start, stop, body):
    def step(i, carry):
        body(i)
        return carry

    LOOP(start, stop, step, 0)


class Gather:
    def __init__(self, place, buf, sems):
        self.p, self.buf = place, buf
        self.zs, self.zr, self.ys, self.yr, self.cs, self.cr = sems

    @staticmethod
    def sems(nz):
        dma = pltpu.SemaphoreType.DMA
        return [
            dma((KVH, nz)), dma((KVH, nz)), dma((KVH, nz)), dma((KVH, nz)),
            dma((KVH, NY, nz)), dma((KVH, NY, nz)),
        ]

    def to_plane(self, g, src_z, dst_z):
        p = self.p
        block = self.buf[g].at[p.tile(src_z, p.y, p.c)]
        return pltpu.make_async_remote_copy(
            block, block, self.zs.at[g, dst_z], self.zr.at[g, src_z],
            device_id=p.at(dst_z, p.y, p.c))

    def to_y(self, g, z, y):
        p = self.p
        block = self.buf[g].at[p.tile(z, y, p.c)]
        return pltpu.make_async_remote_copy(
            block, block, self.ys.at[g, z], self.yr.at[g, z],
            device_id=p.at(p.z, 1 - p.y, p.c))

    def to_core(self, g, z, y, c):
        p = self.p
        block = self.buf[g].at[p.tile(z, y, c)]
        return pltpu.make_async_remote_copy(
            block, block, self.cs.at[g, y, z], self.cr.at[g, y, z],
            device_id=p.at(p.z, p.y, 1 - p.c))

    def first(self, g):
        p = self.p
        self.to_y(g, p.z, p.y).start()
        self.to_core(g, p.z, p.y, p.c).start()
        each(p.z + 1, p.nz, lambda dz: self.to_plane(g, p.z, dz).start())

    def second(self, g):
        p = self.p

        def step(z):
            self.to_plane(g, z, p.z).wait_recv()
            self.to_y(g, z, p.y).start()
            self.to_core(g, z, p.y, p.c).start()

        each(0, p.z, step)

    def third(self, g):
        p = self.p

        def step(z):
            self.to_y(g, z, 1 - p.y).wait_recv()
            self.to_core(g, z, 1 - p.y, p.c).start()

        each(0, p.z + 1, step)

    def fourth(self, g):
        p = self.p

        def step(z):
            self.to_core(g, z, 0, 1 - p.c).wait_recv()
            self.to_core(g, z, 1, 1 - p.c).wait_recv()

        each(0, p.z + 1, step)

    def drain(self, g):
        p = self.p
        each(p.z + 1, p.nz, lambda dz: self.to_plane(g, p.z, dz).wait_send())

        def step(z):
            self.to_y(g, z, p.y).wait_send()
            self.to_core(g, z, 0, p.c).wait_send()
            self.to_core(g, z, 1, p.c).wait_send()

        each(0, p.z + 1, step)


class Reduce:
    def __init__(self, place, part, scratch):
        self.p, self.part = place, part
        (self.for_core, self.kept, self.from_core, self.for_y, self.from_y, self.for_z, self.from_z, self.own,
         self.cs, self.cr, self.ys, self.yr, self.zs, self.zr) = scratch

    @staticmethod
    def scratch(nz):
        dma = pltpu.SemaphoreType.DMA
        block = (2, TILE, HD)
        return [
            pltpu.VMEM((KVH, nz, NY) + block, jnp.bfloat16),
            pltpu.VMEM((KVH, nz, NY) + block, jnp.bfloat16),
            pltpu.VMEM((KVH, nz, NY) + block, jnp.bfloat16),
            pltpu.VMEM((KVH, nz) + block, jnp.bfloat16),
            pltpu.VMEM((KVH, nz) + block, jnp.bfloat16),
            pltpu.VMEM((KVH, nz) + block, jnp.bfloat16),
            pltpu.VMEM((KVH, nz) + block, jnp.bfloat16),
            pltpu.VMEM((KVH,) + block, jnp.float32),
        ] + [dma((KVH, NY, nz))] * 2 + [dma((KVH, nz))] * 4

    def to_core(self, g, z, y):
        p = self.p
        return pltpu.make_async_remote_copy(
            self.for_core.at[g, z, y], self.from_core.at[g, z, y],
            self.cs.at[g, y, z], self.cr.at[g, y, z],
            device_id=p.at(p.z, p.y, 1 - p.c))

    def to_y(self, g, z):
        p = self.p
        return pltpu.make_async_remote_copy(
            self.for_y.at[g, z], self.from_y.at[g, z], self.ys.at[g, z], self.yr.at[g, z],
            device_id=p.at(p.z, 1 - p.y, p.c))

    def to_plane(self, g, src_z, dst_z):
        p = self.p
        return pltpu.make_async_remote_copy(
            self.for_z.at[g, dst_z], self.from_z.at[g, src_z],
            self.zs.at[g, dst_z], self.zr.at[g, src_z],
            device_id=p.at(dst_z, p.y, p.c))

    def first(self, g, slot_of):
        p = self.p

        def block(z, y, c):
            slot = slot_of[p.tile(z, y, c)]
            values = self.part[jnp.maximum(slot, 0)]
            return jnp.where(slot >= 0, values, jnp.zeros_like(values))

        def step(z):
            for y in (1 - p.y, p.y):
                self.for_core[g, z, y] = block(z, y, 1 - p.c)
                self.to_core(g, z, y).start()
            for y in range(NY):
                self.kept[g, z, y] = block(z, y, p.c)

        each(0, p.z + 1, step)

    def second(self, g):
        p = self.p

        def step(z):
            y = 1 - p.y
            self.to_core(g, z, y).wait_recv()
            total = self.kept[g, z, y].astype(jnp.float32) + self.from_core[g, z, y].astype(jnp.float32)
            self.for_y[g, z] = total.astype(jnp.bfloat16)
            self.to_y(g, z).start()

        each(0, p.z + 1, step)

    def third(self, g):
        p = self.p

        def total(z):
            self.to_core(g, z, p.y).wait_recv()
            self.to_y(g, z).wait_recv()
            return (
                self.kept[g, z, p.y].astype(jnp.float32)
                + self.from_core[g, z, p.y].astype(jnp.float32)
                + self.from_y[g, z].astype(jnp.float32)
            )

        def step(z):
            self.for_z[g, z] = total(z).astype(jnp.bfloat16)
            self.to_plane(g, p.z, z).start()

        each(0, p.z, step)
        self.own[g] = total(p.z)

    def fourth(self, g):
        p = self.p

        def step(z):
            self.to_plane(g, z, p.z).wait_recv()
            self.own[g] += self.from_z[g, z].astype(jnp.float32)

        each(p.z + 1, p.nz, step)

    def drain(self, g):
        p = self.p

        def step(z):
            self.to_core(g, z, 0).wait_send()
            self.to_core(g, z, 1).wait_send()
            self.to_y(g, z).wait_send()

        each(0, p.z + 1, step)
        each(0, p.z, lambda z: self.to_plane(g, p.z, z).wait_send())


def dot(a, b):
    return jnp.dot(a, b, preferred_element_type=jnp.float32)


def fold(x, op):
    return op(x.reshape(TILE // 8, 8, x.shape[-1]), axis=0)


HALVES = (slice(0, TILE), slice(TILE, 2 * TILE))


def backward_kernel(
    tiles, pairs, table, slot_of, k_ref, v_ref, q_ref, o_ref, g_ref, dq_ref, dk_ref, dv_ref,
    qt, qs, gt, gs, delta, scores, slopes, peak, total, dqt, part, *rest,
):
    place = Place(tiles)
    buf, rest = rest[:KVH], rest[KVH:]
    gather = Gather(place, buf, rest[:6])
    reduce = Reduce(place, part, rest[6:])

    def head_columns(g):
        return slice(g * HD, (g + 1) * HD)

    for g in range(KVH):
        buf[g][place.me, 0] = k_ref[:, head_columns(g)]
        buf[g][place.me, 1] = v_ref[:, head_columns(g)]
    place.meet()

    def prepare(g):
        for h in range(GROUP):
            rows = slice(h * TILE, (h + 1) * TILE)
            columns = slice(g * ROWS + h * TILE, g * ROWS + (h + 1) * TILE)
            q, go = q_ref[:, columns], g_ref[:, columns]
            qs[rows, :] = q
            gs[rows, :] = go
            qt[:, rows] = q.T
            gt[:, rows] = go.T
            product = go.astype(jnp.float32) * o_ref[:, columns].astype(jnp.float32)
            delta[:, rows] = jnp.sum(product.T, axis=0, keepdims=True)
        s = dot(k_ref[:, head_columns(g)], qt[...])
        key_pos = lax.broadcasted_iota(jnp.int32, s.shape, 0)
        query_pos = lax.broadcasted_iota(jnp.int32, s.shape, 1) & (TILE - 1)
        s = jnp.where(key_pos <= query_pos, s, -1e30)
        scores[0] = s
        peak[...] = fold(s, jnp.max)
        slopes[0] = dot(v_ref[:, head_columns(g)], gt[...]) - delta[...]

    def tile_pair(g, i, which):
        return jnp.concatenate(
            [buf[g][jnp.maximum(table[2 * i + j], 0), which] for j in range(2)], axis=0
        )

    def score(g, i):
        s = dot(tile_pair(g, i, 0), qt[...])
        for j, half in enumerate(HALVES):
            scores[1 + 2 * i + j] = s[half]
            bias = jnp.where(table[2 * i + j] >= 0, 0.0, -1e30)
            peak[...] = jnp.maximum(peak[...], fold(s[half], jnp.max) + bias)

    def weigh_self(top):
        w = jnp.exp2((scores[0] - top) * EXP_SCALE)
        scores[0] = w
        total[...] = fold(w, jnp.sum)

    def weigh(g, i, top):
        slope = dot(tile_pair(g, i, 1), gt[...])
        for j, half in enumerate(HALVES):
            slot = 1 + 2 * i + j
            w = jnp.exp2((scores[slot] - top) * EXP_SCALE)
            w = jnp.where(table[2 * i + j] >= 0, w, 0.0)
            scores[slot] = w
            total[...] += fold(w, jnp.sum)
            slopes[slot] = slope[half] - delta[...]

    def back_self(g, inverse):
        p = scores[0] * inverse
        ds = (p * slopes[0]).astype(jnp.bfloat16)
        part[0, 1] = dot(p.astype(jnp.bfloat16), gs[...]).astype(jnp.bfloat16)
        part[0, 0] = (dot(ds, qs[...]) * SCALE).astype(jnp.bfloat16)
        dqt[...] = dot(k_ref[:, head_columns(g)].T, ds)

    def back(g, i, inverse):
        first = 1 + 2 * i
        p = scores[pl.ds(first, 2)].reshape(2 * TILE, ROWS) * inverse
        ds = (p * slopes[pl.ds(first, 2)].reshape(2 * TILE, ROWS)).astype(jnp.bfloat16)
        dv = dot(p.astype(jnp.bfloat16), gs[...]).astype(jnp.bfloat16)
        dk = (dot(ds, qs[...]) * SCALE).astype(jnp.bfloat16)
        for j, half in enumerate(HALVES):
            part[first + j, 0] = dk[half]
            part[first + j, 1] = dv[half]
        dqt[...] += dot(tile_pair(g, i, 0).T, ds)

    gather.first(0)
    gather.first(1)
    prepare(0)
    gather.second(0)
    gather.first(2)
    gather.third(0)
    gather.second(1)
    gather.first(3)
    for g in range(KVH):
        if g:
            prepare(g)
        gather.fourth(g)
        each(0, pairs, functools.partial(score, g))
        if g + 1 < KVH:
            gather.third(g + 1)
        if g:
            reduce.second(g - 1)
        top = jnp.max(peak[...], axis=0, keepdims=True)
        weigh_self(top)
        each(0, pairs, lambda i: weigh(g, i, top))
        if g + 2 < KVH:
            gather.second(g + 2)
        if g:
            reduce.third(g - 1)
        inverse = 1.0 / jnp.sum(total[...], axis=0, keepdims=True)
        back_self(g, inverse)
        each(0, pairs, lambda i: back(g, i, inverse))
        reduce.first(g, slot_of)
        for h in range(GROUP):
            rows = slice(h * TILE, (h + 1) * TILE)
            columns = slice(g * ROWS + h * TILE, g * ROWS + (h + 1) * TILE)
            dq_ref[:, columns] = (dqt[:, rows].T * SCALE).astype(jnp.bfloat16)
    reduce.second(KVH - 1)
    reduce.third(KVH - 1)
    for g in range(KVH):
        reduce.fourth(g)
        dk_ref[:, head_columns(g)] = reduce.own[g, 0].astype(jnp.bfloat16)
        dv_ref[:, head_columns(g)] = reduce.own[g, 1].astype(jnp.bfloat16)
    for g in range(KVH):
        gather.drain(g)
        reduce.drain(g)


def per_device(tiles, queries, keys, values, outputs, out_grad, ancestors):
    depth = ancestors.shape[1]
    pairs = (depth + 1) // 2
    slots = 1 + 2 * pairs
    nz = tiles // (NY * NC)
    me = lax.axis_index("tok").astype(jnp.int32)
    row = lax.dynamic_slice_in_dim(ancestors, me, 1, 0)[0]
    table = jnp.pad(row, (0, 2 * pairs - depth), constant_values=-1)
    listed = jnp.concatenate([me[None], table])
    match = listed[None, :] == jnp.arange(tiles, dtype=jnp.int32)[:, None]
    slot_of = jnp.max(jnp.where(match, jnp.arange(slots, dtype=jnp.int32)[None, :], -1), axis=1)
    vmem = pl.BlockSpec(memory_space=pltpu.VMEM)
    smem = pl.BlockSpec(memory_space=pltpu.SMEM)
    f32, bf16 = jnp.float32, jnp.bfloat16
    return pl.pallas_call(
        functools.partial(backward_kernel, tiles, pairs),
        out_shape=(
            jax.ShapeDtypeStruct(queries.shape, bf16),
            jax.ShapeDtypeStruct(keys.shape, bf16),
            jax.ShapeDtypeStruct(values.shape, bf16),
        ),
        in_specs=[smem] * 2 + [vmem] * 5,
        out_specs=(vmem,) * 3,
        scratch_shapes=[
            pltpu.VMEM((HD, ROWS), bf16),
            pltpu.VMEM((ROWS, HD), bf16),
            pltpu.VMEM((HD, ROWS), bf16),
            pltpu.VMEM((ROWS, HD), bf16),
            pltpu.VMEM((1, ROWS), f32),
            pltpu.VMEM((slots, TILE, ROWS), f32),
            pltpu.VMEM((slots, TILE, ROWS), f32),
            pltpu.VMEM((8, ROWS), f32),
            pltpu.VMEM((8, ROWS), f32),
            pltpu.VMEM((HD, ROWS), f32),
            pltpu.VMEM((slots, 2, TILE, HD), bf16),
        ]
        + [pltpu.VMEM((tiles, 2, TILE, HD), bf16)] * KVH
        + Gather.sems(nz)
        + Reduce.scratch(nz),
        compiler_params=pltpu.CompilerParams(
            collective_id=0, has_side_effects=True, vmem_limit_bytes=60 << 20),
    )(table, slot_of, keys, values, queries, outputs, out_grad)


def solution(mesh):
    rows = P(("parts", "tok"), None)
    return jax.shard_map(
        functools.partial(per_device, mesh.shape["tok"]),
        mesh=mesh,
        in_specs=(rows,) * 5 + (P("parts", None),),
        out_specs=(rows,) * 3,
        check_vma=False,
    )
```

time: 119 us -> 93.9 us (0.79)
  Pallas kernels: 111 us -> 87.2 us
  local copies, waits for them, and re-layouts: 3.14 us -> 5.06 us
  other arithmetic: 1.93 us -> 0.7 us
    pallas_call x3 -> x1, Pallas kernels: 111 us -> 87.2 us  [per_device(): pl.pallas_call(functools.partial(backward_kernel, tiles, pairs), out_shap...]
    unnamed x2 -> x11, local copies, waits for them, and re-layouts: 3.14 us -> 5.06 us
    reduce_sum x1 -> x0, other arithmetic: 1.33 us -> none  [per_device(): jnp.sum((row >= 0).astype(jnp.int32))]
where the time goes in v2:
time: 93.9 us; the launch traced here: 93.7 us
  Pallas kernels  87.2 us (93%)
  local copies, waits for them, and re-layouts  5.06 us (5%)
    pallas_call x1, Pallas kernels, per_device(): pl.pallas_call(functools.partial(backward_kernel, tiles, pairs), out_shap...  87.2 us
    unnamed x11, local copies, waits for them, and re-layouts  5.06 us

profile of v2, /device:TPU:0, one launch (start us, length us, event | category | flops | bytes accessed | tf_op | source)
XLA Modules:
  0.0 93.7 jit_solution(1401234840414014745)
XLA Ops:
  0.6 0.0 copy-start
  0.6 0.7 copy-done
  1.3 0.0 copy-start.3
  1.3 0.1 pad_add_fusion
  1.4 0.4 copy-done.3
  1.9 0.6 select_reduce_fusion.slot_of
  2.5 87.2 %shard_map.85 = (bf16[128,4096]{1,0:T(8,128)(2,1)}, bf16[128,512]{1,0:T(8,128)(2,1)}, bf16[128,512]{1,0:T(8,128)(2,1)}) custom-call(s32[10]{0:T(128)} %copy-done.3, s32[16]{0:T(128)} %select_reduce_fusion.slot_of, bf16[128,512]{1,0:T(8,128)(2,1)} %k_ref.1, bf16[128,512]{1,0:T(8,128)(2,1)} %v_ref.1, bf16[128,4096]{1,0:T(8,128)(2,1)} %q_ref.1, ...), custom_call_target="tpu_custom_call" | custom-call | tf_op jit(solution)/shard_map/pallas_call | solution.py:401
  89.7 0.0 copy-start.2
  89.7 2.3 %copy.12 = bf16[128,4096]{1,0:T(8,128)(2,1)} copy(bf16[128,4096]{1,0:T(8,128)(2,1)} %get-tuple-element.6) | data formatting | bytes 2097152
  92.1 0.0 copy-done.2
  92.1 0.0 copy-start.1
  92.1 0.7 copy.13
  92.7 0.3 copy-done.1
  93.0 0.7 copy.14
  (1 shorter events, 0.0 us)
Async XLA Ops:
  0.6 0.7 copy-start
  1.3 0.5 copy-start.3
  89.7 2.3 %copy-start.2 = (bf16[128,512]{1,0:T(8,128)(2,1)S(1)}, bf16[128,512]{1,0:T(8,128)(2,1)}, u32[]{:S(2)}) copy-start(bf16[128,512]{1,0:T(8,128)(2,1)} %get-tuple-element.7) | copy-start | bytes 393220
  92.1 1.0 %copy-start.1 = (bf16[128,512]{1,0:T(8,128)(2,1)S(1)}, bf16[128,512]{1,0:T(8,128)(2,1)}, u32[]{:S(2)}) copy-start(bf16[128,512]{1,0:T(8,128)(2,1)} %get-tuple-element.8) | copy-start | bytes 393220

commit v3 on v2

--- a/solution.py
+++ b/solution.py
@@ -95,14 +95,15 @@
 
     def first(self, g):
         p = self.p
-        self.to_y(g, p.z, p.y).start()
+        pl.when(p.y == 0)(lambda: self.to_y(g, p.z, p.y).start())
         self.to_core(g, p.z, p.y, p.c).start()
         each(p.z + 1, p.nz, lambda dz: self.to_plane(g, p.z, dz).start())
 
     def second(self, g):
         p = self.p
 
-        def step(z):
+        def step(i):
+            z = p.z - 1 - i
             self.to_plane(g, z, p.z).wait_recv()
             self.to_y(g, z, p.y).start()
             self.to_core(g, z, p.y, p.c).start()
@@ -112,31 +113,24 @@
     def third(self, g):
         p = self.p
 
-        def step(z):
+        def step(i):
+            z = p.z - i
             self.to_y(g, z, 1 - p.y).wait_recv()
             self.to_core(g, z, 1 - p.y, p.c).start()
 
-        each(0, p.z + 1, step)
+        each(1 - p.y, p.z + 1, step)
 
     def fourth(self, g):
         p = self.p
-
-        def step(z):
-            self.to_core(g, z, 0, 1 - p.c).wait_recv()
-            self.to_core(g, z, 1, 1 - p.c).wait_recv()
-
-        each(0, p.z + 1, step)
+        each(0, p.z + 1, lambda z: self.to_core(g, z, p.y, 1 - p.c).wait_recv())
+        each(0, p.z + p.y, lambda z: self.to_core(g, z, 1 - p.y, 1 - p.c).wait_recv())
 
     def drain(self, g):
         p = self.p
         each(p.z + 1, p.nz, lambda dz: self.to_plane(g, p.z, dz).wait_send())
-
-        def step(z):
-            self.to_y(g, z, p.y).wait_send()
-            self.to_core(g, z, 0, p.c).wait_send()
-            self.to_core(g, z, 1, p.c).wait_send()
-
-        each(0, p.z + 1, step)
+        each(0, p.z + 1 - p.y, lambda z: self.to_y(g, z, p.y).wait_send())
+        each(0, p.z + 1, lambda z: self.to_core(g, z, p.y, p.c).wait_send())
+        each(0, p.z + p.y, lambda z: self.to_core(g, z, 1 - p.y, p.c).wait_send())
 
 
 class Reduce:
@@ -188,14 +182,20 @@
             values = self.part[jnp.maximum(slot, 0)]
             return jnp.where(slot >= 0, values, jnp.zeros_like(values))
 
-        def step(z):
-            for y in (1 - p.y, p.y):
+        def give(y):
+            def step(z):
                 self.for_core[g, z, y] = block(z, y, 1 - p.c)
                 self.to_core(g, z, y).start()
+
+            return step
+
+        def keep(z):
             for y in range(NY):
                 self.kept[g, z, y] = block(z, y, p.c)
 
-        each(0, p.z + 1, step)
+        each(0, p.z + p.y, give(1 - p.y))
+        each(0, p.z + 1, give(p.y))
+        each(0, p.z + 1, keep)
 
     def second(self, g):
         p = self.p
@@ -207,26 +207,29 @@
             self.for_y[g, z] = total.astype(jnp.bfloat16)
             self.to_y(g, z).start()
 
-        each(0, p.z + 1, step)
+        each(0, p.z + p.y, step)
 
     def third(self, g):
         p = self.p
 
-        def total(z):
+        def mine(z):
             self.to_core(g, z, p.y).wait_recv()
+            return self.kept[g, z, p.y].astype(jnp.float32) + self.from_core[g, z, p.y].astype(jnp.float32)
+
+        def across(z):
             self.to_y(g, z).wait_recv()
-            return (
-                self.kept[g, z, p.y].astype(jnp.float32)
-                + self.from_core[g, z, p.y].astype(jnp.float32)
-                + self.from_y[g, z].astype(jnp.float32)
-            )
+            return self.from_y[g, z].astype(jnp.float32)
 
         def step(z):
-            self.for_z[g, z] = total(z).astype(jnp.bfloat16)
+            self.for_z[g, z] = (mine(z) + across(z)).astype(jnp.bfloat16)
             self.to_plane(g, p.z, z).start()
 
         each(0, p.z, step)
-        self.own[g] = total(p.z)
+        self.own[g] = mine(p.z)
+
+        @pl.when(p.y == 0)
+        def _():
+            self.own[g] += across(p.z)
 
     def fourth(self, g):
         p = self.p
@@ -239,13 +242,9 @@
 
     def drain(self, g):
         p = self.p
-
-        def step(z):
-            self.to_core(g, z, 0).wait_send()
-            self.to_core(g, z, 1).wait_send()
-            self.to_y(g, z).wait_send()
-
-        each(0, p.z + 1, step)
+        each(0, p.z + 1, lambda z: self.to_core(g, z, p.y).wait_send())
+        each(0, p.z + p.y, lambda z: self.to_core(g, z, 1 - p.y).wait_send())
+        each(0, p.z + p.y, lambda z: self.to_y(g, z).wait_send())
         each(0, p.z, lambda z: self.to_plane(g, p.z, z).wait_send())
 
 
@@ -253,6 +252,11 @@
     return jnp.dot(a, b, preferred_element_type=jnp.float32)
 
 
+def dot_last(a, b):
+    return lax.dot_general(
+        a, b, (((1,), (1,)), ((), ())), preferred_element_type=jnp.float32)
+
+
 def fold(x, op):
     return op(x.reshape(TILE // 8, 8, x.shape[-1]), axis=0)
 
@@ -262,7 +266,7 @@
 
 def backward_kernel(
     tiles, pairs, table, slot_of, k_ref, v_ref, q_ref, o_ref, g_ref, dq_ref, dk_ref, dv_ref,
-    qt, qs, gt, gs, delta, scores, slopes, peak, total, dqt, part, *rest,
+    qs, gs, delta, scores, slopes, peak, total, dqt, part, *rest,
 ):
     place = Place(tiles)
     buf, rest = rest[:KVH], rest[KVH:]
@@ -277,24 +281,26 @@
         buf[g][place.me, 1] = v_ref[:, head_columns(g)]
     place.meet()
 
-    def prepare(g):
-        for h in range(GROUP):
-            rows = slice(h * TILE, (h + 1) * TILE)
-            columns = slice(g * ROWS + h * TILE, g * ROWS + (h + 1) * TILE)
-            q, go = q_ref[:, columns], g_ref[:, columns]
-            qs[rows, :] = q
-            gs[rows, :] = go
-            qt[:, rows] = q.T
-            gt[:, rows] = go.T
-            product = go.astype(jnp.float32) * o_ref[:, columns].astype(jnp.float32)
-            delta[:, rows] = jnp.sum(product.T, axis=0, keepdims=True)
-        s = dot(k_ref[:, head_columns(g)], qt[...])
+    def stack(h, carry):
+        rows = pl.ds(pl.multiple_of(h * TILE, TILE), TILE)
+        q, go = q_ref[:, rows], g_ref[:, rows]
+        qs[rows, :] = q
+        gs[rows, :] = go
+        product = go.astype(jnp.float32) * o_ref[:, rows].astype(jnp.float32)
+        delta[:, rows] = jnp.sum(product.T, axis=0, keepdims=True)
+        return carry
+
+    def head_rows(g):
+        return slice(g * ROWS, (g + 1) * ROWS)
+
+    def self_score(g):
+        s = dot_last(k_ref[:, head_columns(g)], qs[head_rows(g), :])
         key_pos = lax.broadcasted_iota(jnp.int32, s.shape, 0)
         query_pos = lax.broadcasted_iota(jnp.int32, s.shape, 1) & (TILE - 1)
         s = jnp.where(key_pos <= query_pos, s, -1e30)
         scores[0] = s
         peak[...] = fold(s, jnp.max)
-        slopes[0] = dot(v_ref[:, head_columns(g)], gt[...]) - delta[...]
+        slopes[0] = dot_last(v_ref[:, head_columns(g)], gs[head_rows(g), :]) - delta[:, head_rows(g)]
 
     def tile_pair(g, i, which):
         return jnp.concatenate(
@@ -302,7 +308,7 @@
         )
 
     def score(g, i):
-        s = dot(tile_pair(g, i, 0), qt[...])
+        s = dot_last(tile_pair(g, i, 0), qs[head_rows(g), :])
         for j, half in enumerate(HALVES):
             scores[1 + 2 * i + j] = s[half]
             bias = jnp.where(table[2 * i + j] >= 0, 0.0, -1e30)
@@ -314,46 +320,50 @@
         total[...] = fold(w, jnp.sum)
 
     def weigh(g, i, top):
-        slope = dot(tile_pair(g, i, 1), gt[...])
+        slope = dot_last(tile_pair(g, i, 1), gs[head_rows(g), :])
         for j, half in enumerate(HALVES):
             slot = 1 + 2 * i + j
             w = jnp.exp2((scores[slot] - top) * EXP_SCALE)
             w = jnp.where(table[2 * i + j] >= 0, w, 0.0)
             scores[slot] = w
             total[...] += fold(w, jnp.sum)
-            slopes[slot] = slope[half] - delta[...]
+            slopes[slot] = slope[half] - delta[:, head_rows(g)]
 
     def back_self(g, inverse):
         p = scores[0] * inverse
         ds = (p * slopes[0]).astype(jnp.bfloat16)
-        part[0, 1] = dot(p.astype(jnp.bfloat16), gs[...]).astype(jnp.bfloat16)
-        part[0, 0] = (dot(ds, qs[...]) * SCALE).astype(jnp.bfloat16)
+        part[0, 1] = dot(p.astype(jnp.bfloat16), gs[head_rows(g), :]).astype(jnp.bfloat16)
+        part[0, 0] = (dot(ds, qs[head_rows(g), :]) * SCALE).astype(jnp.bfloat16)
         dqt[...] = dot(k_ref[:, head_columns(g)].T, ds)
 
     def back(g, i, inverse):
         first = 1 + 2 * i
         p = scores[pl.ds(first, 2)].reshape(2 * TILE, ROWS) * inverse
         ds = (p * slopes[pl.ds(first, 2)].reshape(2 * TILE, ROWS)).astype(jnp.bfloat16)
-        dv = dot(p.astype(jnp.bfloat16), gs[...]).astype(jnp.bfloat16)
-        dk = (dot(ds, qs[...]) * SCALE).astype(jnp.bfloat16)
+        dv = dot(p.astype(jnp.bfloat16), gs[head_rows(g), :]).astype(jnp.bfloat16)
+        dk = (dot(ds, qs[head_rows(g), :]) * SCALE).astype(jnp.bfloat16)
         for j, half in enumerate(HALVES):
             part[first + j, 0] = dk[half]
             part[first + j, 1] = dv[half]
         dqt[...] += dot(tile_pair(g, i, 0).T, ds)
 
     gather.first(0)
+    LOOP(0, 2 * GROUP, stack, 0)
     gather.first(1)
-    prepare(0)
+    LOOP(2 * GROUP, KVH * GROUP, stack, 0)
+    gather.first(2)
+    self_score(0)
     gather.second(0)
-    gather.first(2)
+    gather.first(3)
     gather.third(0)
     gather.second(1)
-    gather.first(3)
     for g in range(KVH):
         if g:
-            prepare(g)
+            self_score(g)
         gather.fourth(g)
         each(0, pairs, functools.partial(score, g))
+        if g == 0:
+            gather.second(2)
         if g + 1 < KVH:
             gather.third(g + 1)
         if g:
@@ -361,14 +371,14 @@
         top = jnp.max(peak[...], axis=0, keepdims=True)
         weigh_self(top)
         each(0, pairs, lambda i: weigh(g, i, top))
-        if g + 2 < KVH:
-            gather.second(g + 2)
-        if g:
-            reduce.third(g - 1)
+        if g == 0:
+            gather.second(3)
         inverse = 1.0 / jnp.sum(total[...], axis=0, keepdims=True)
         back_self(g, inverse)
         each(0, pairs, lambda i: back(g, i, inverse))
         reduce.first(g, slot_of)
+        if g:
+            reduce.third(g - 1)
         for h in range(GROUP):
             rows = slice(h * TILE, (h + 1) * TILE)
             columns = slice(g * ROWS + h * TILE, g * ROWS + (h + 1) * TILE)
@@ -408,11 +418,9 @@
         in_specs=[smem] * 2 + [vmem] * 5,
         out_specs=(vmem,) * 3,
         scratch_shapes=[
-            pltpu.VMEM((HD, ROWS), bf16),
-            pltpu.VMEM((ROWS, HD), bf16),
-            pltpu.VMEM((HD, ROWS), bf16),
-            pltpu.VMEM((ROWS, HD), bf16),
-            pltpu.VMEM((1, ROWS), f32),
+            pltpu.VMEM((KVH * ROWS, HD), bf16),
+            pltpu.VMEM((KVH * ROWS, HD), bf16),
+            pltpu.VMEM((1, KVH * ROWS), f32),
             pltpu.VMEM((slots, TILE, ROWS), f32),
             pltpu.VMEM((slots, TILE, ROWS), f32),
             pltpu.VMEM((8, ROWS), f32),

time: 93.9 us -> 78.9 us (0.84)
  Pallas kernels: 87.2 us -> 72.2 us
    pallas_call x1, Pallas kernels: 87.2 us -> 72.2 us  [per_device(): pl.pallas_call(functools.partial(backward_kernel, tiles, pairs), out_shap...]
where the time goes in v3:
time: 78.9 us; the launch traced here: 78.7 us
  Pallas kernels  72.2 us (92%)
  local copies, waits for them, and re-layouts  5.06 us (6%)
    pallas_call x1, Pallas kernels, per_device(): pl.pallas_call(functools.partial(backward_kernel, tiles, pairs), out_shap...  72.2 us
    unnamed x11, local copies, waits for them, and re-layouts  5.06 us

profile of v3, /device:TPU:0, one launch (start us, length us, event | category | flops | bytes accessed | tf_op | source)
XLA Modules:
  0.0 78.7 jit_solution(17795926508078453492)
XLA Ops:
  0.6 0.0 copy-start
  0.6 0.7 copy-done
  1.3 0.0 copy-start.3
  1.3 0.1 pad_add_fusion
  1.4 0.4 copy-done.3
  1.9 0.6 select_reduce_fusion.slot_of
  2.5 72.2 %shard_map.85 = (bf16[128,4096]{1,0:T(8,128)(2,1)}, bf16[128,512]{1,0:T(8,128)(2,1)}, bf16[128,512]{1,0:T(8,128)(2,1)}) custom-call(s32[10]{0:T(128)} %copy-done.3, s32[16]{0:T(128)} %select_reduce_fusion.slot_of, bf16[128,512]{1,0:T(8,128)(2,1)} %k_ref.1, bf16[128,512]{1,0:T(8,128)(2,1)} %v_ref.1, bf16[128,4096]{1,0:T(8,128)(2,1)} %q_ref.1, ...), custom_call_target="tpu_custom_call" | custom-call | tf_op jit(solution)/shard_map/pallas_call | solution.py:411
  74.7 0.0 copy-start.2
  74.7 2.3 %copy.12 = bf16[128,4096]{1,0:T(8,128)(2,1)} copy(bf16[128,4096]{1,0:T(8,128)(2,1)} %get-tuple-element.6) | data formatting | bytes 2097152
  77.0 0.0 copy-done.2
  77.0 0.0 copy-start.1
  77.1 0.7 copy.13
  77.7 0.3 copy-done.1
  78.0 0.7 copy.14
  (1 shorter events, 0.0 us)
Async XLA Ops:
  0.6 0.7 copy-start
  1.3 0.5 copy-start.3
  74.7 2.3 %copy-start.2 = (bf16[128,512]{1,0:T(8,128)(2,1)S(1)}, bf16[128,512]{1,0:T(8,128)(2,1)}, u32[]{:S(2)}) copy-start(bf16[128,512]{1,0:T(8,128)(2,1)} %get-tuple-element.7) | copy-start | bytes 393220
  77.0 1.0 %copy-start.1 = (bf16[128,512]{1,0:T(8,128)(2,1)S(1)}, bf16[128,512]{1,0:T(8,128)(2,1)}, u32[]{:S(2)}) copy-start(bf16[128,512]{1,0:T(8,128)(2,1)} %get-tuple-element.8) | copy-start | bytes 393220
